TPU v7x, 256 devices: a whole 4x4x8 slice. The times are simulated.
256 devices in a mesh: frames: 16 (over y, x), pix: 16 (over z, core).
Axes of the slice: x: 4, y: 4, z: 8, core: 2. Of those that a mesh axis runs over, the one named last changes fastest.
Arguments:
- photon_counts: int32 [16384, 32768], P('frames', 'pix'), may hold values from 1 to 53, as said below
- flat_field: float32 [32768], P('pix'), may hold values from 0.5 to 2
- owner_counts: int32 [16], replicated, may hold values from 512 to 2048, as said below
Outputs:
- diagonal_tiles: float32 [16384, 1024], P(('frames', 'pix'))
- offdiag_tiles: float32 [16384, 1024], P(('frames', 'pix'))
Inputs may be any that keep to these rules, and one draw needn't show every extreme that they name: owner_counts[i] is how many of owner i's 2048 slots, the first ones, hold cycle pixels; some owner holds all 2048. `photon_counts`: whole photon counts of each slot in each frame.
All inputs are finite; a program needn't handle non-finite values.
Results may differ from a plain program's by a relative error of at most 0.0003.
Values may be sent and summed in bfloat16 or wider, within the bound.
No kernel may reach another device: no remote copies, remote signals or barrier semaphores. Data moves between devices by JAX's collectives and lax.ppermute only.
A program may use at most 64 MiB of HBM per device.

v0:
```python
import jax
import jax.numpy as jnp
from jax import lax
from jax.sharding import PartitionSpec as P


def shifted(value, axis, steps):
    count = lax.axis_size(axis)
    leading, last = (max(0, -steps), min(count, count - steps))
    return lax.ppermute(value, axis, [(source, source + steps) for source in range(leading, last)])


def gram(left, right):
    return lax.dot_general(
        left, right, (((1,), (1,)), ((), ())), preferred_element_type=jnp.float32
    )


def on_device(photon_counts, flat_field, owner_counts):
    owner_index = lax.axis_index("pix")
    slot_count = flat_field.shape[0]
    limit = owner_counts[owner_index]
    valid = (jnp.arange(slot_count, dtype=jnp.int32) < limit).astype(jnp.float32)
    weights = flat_field * valid
    pixel_total = jnp.sum(owner_counts).astype(jnp.float32)
    corrected = photon_counts.astype(jnp.float32) * weights[None, :]
    frame_sums = lax.psum(jnp.sum(corrected, axis=1), "pix")
    frame_mean = frame_sums / pixel_total
    scaled = (corrected / frame_mean[:, None]).astype(jnp.bfloat16)
    earlier = shifted(scaled, "frames", 1)
    diagonal_part = gram(scaled, scaled)
    offdiag_part = gram(scaled, earlier)
    diagonal_rows, offdiag_rows = (
        lax.psum_scatter(diagonal_part, "pix", scatter_dimension=0, tiled=True),
        lax.psum_scatter(offdiag_part, "pix", scatter_dimension=0, tiled=True),
    )
    return (diagonal_rows / pixel_total, offdiag_rows / pixel_total)


def solution(mesh):
    placed = (P("frames", "pix"), P("pix"), P())
    return jax.shard_map(
        on_device,
        mesh=mesh,
        in_specs=placed,
        out_specs=(P(("frames", "pix"), None), P(("frames", "pix"), None)),
        check_vma=False,
    )
```

profile of v0, /device:TPU:4, one launch (start us, length us, event | category | flops | bytes accessed | tf_op | source)
XLA Modules:
  0.0 229.9 jit_solution(11352595881727451091)
XLA Ops:
  7.2 0.0 reduce-scatter.3.cloned.1.call-start
  7.2 1.3 reduce_sum.19
  8.5 1.2 dynamic_slice.3
  9.7 1.3 fusion.1
  11.1 4.3 %fusion = f32[1024]{0:T(1024)S(1)} fusion(s32[1024,2048]{1,0:T(8,128)} %param.3, f32[2048]{0:T(1024)S(1)} %fusion.1), kind=kLoop, calls=%fused_computation.2 | loop fusion | flops 6290432 | bytes 8400896 | tf_op jit(solution)/shard_map/reduce_sum | solution.py:27
  15.4 28.8 %psum.7 = f32[1024]{0:T(1024)S(1)} all-reduce(f32[1024]{0:T(1024)S(1)} %fusion), channel_id=1, replica_groups=mesh['frames'=16,'pix'=16] {'pix'}, use_global_device_ids=true, to_apply=%region_1.0 | all-reduce | flops 1024 | bytes 8192 | tf_op jit(solution)/shard_map/psum | solution.py:27
  44.9 4.3 %divide_convert_fusion = bf16[1024,2048]{1,0:T(8,128)(2,1)S(1)} fusion(s32[1024,2048]{1,0:T(8,128)} %param.3, f32[1024]{0:T(1024)S(1)} %broadcast_divide_fusion.2, f32[2048]{0:T(1024)S(1)} %fusion.1), kind=kLoop, calls=%fused_computation | loop fusion | flops 8388608 | bytes 12595200 | tf_op jit(solution)/shard_map/convert_element_type | solution.py:29
  49.2 0.0 copy-start
  49.2 2.0 copy-done
  51.2 6.1 %fusion.2 = f32[1024,1024]{1,0:T(8,128)} fusion(bf16[1024,2048]{1,0:T(8,128)(2,1)S(1)} %divide_convert_fusion), kind=kOutput, calls=%fused_computation.8 | convolution fusion | flops 4294967296 | bytes 8388608 | tf_op jit(solution)/shard_map/dot_general | solution.py:14
  57.3 0.0 reduce-scatter.3.cloned.1.call-update
  57.3 0.0 reduce-scatter.5.cloned.1.call-start
  57.3 3.1 %collective-permute-start = (bf16[1024,2048]{1,0:T(8,128)(2,1)}, bf16[1024,2048]{1,0:T(8,128)(2,1)S(1)}, u32[]{:S(2)}, u32[]{:S(2)}) collective-permute-start(bf16[1024,2048]{1,0:T(8,128)(2,1)} %copy-done), channel_id=1, source_target_pairs={{0,16},{16,32},{32,48},{48,64},{64,80},{80,96},{96,112},{112,128},... | collective-permute-start | bytes 12582920 | tf_op jit(solution)/shard_map/ppermute | solution.py:10
  60.4 89.1 %collective-permute-done = bf16[1024,2048]{1,0:T(8,128)(2,1)S(1)} collective-permute-done((bf16[1024,2048]{1,0:T(8,128)(2,1)}, bf16[1024,2048]{1,0:T(8,128)(2,1)S(1)}, u32[]{:S(2)}, u32[]{:S(2)}) %collective-permute-start) | collective-permute-done | bytes 4194336 | tf_op jit(solution)/shard_map/ppermute | solution.py:10
  149.5 8.4 %fusion.3 = f32[1024,1024]{1,0:T(8,128)} fusion(bf16[1024,2048]{1,0:T(8,128)(2,1)} %copy-done, bf16[1024,2048]{1,0:T(8,128)(2,1)S(1)} %collective-permute-done), kind=kOutput, calls=%fused_computation.9 | convolution fusion | flops 4294967296 | bytes 12582912 | tf_op jit(solution)/shard_map/dot_general | solution.py:14
  157.9 0.0 reduce-scatter.5.cloned.1.call-update
  157.9 0.0 reduce-scatter.3.cloned.1.call-done
  157.9 1.7 broadcast_divide_fusion.1
  159.6 61.8 %reduce-scatter.5.cloned.1.call-done = f32[64,1024]{1,0:T(8,128)} async-done(((f32[1024,1024]{1,0:T(8,128)}), f32[64,1024]{1,0:T(8,128)}) %reduce-scatter.5.cloned.1.call-update) | async-done | bytes 262160 | tf_op jit(solution)/shard_map/reduce_scatter | solution.py:35
  221.4 1.7 broadcast_divide_fusion
  (1 shorter events, 0.0 us)
Async XLA Ops:
  7.2 150.8 %reduce-scatter.3.cloned.1.call-start = ((), (), s32[]{:S(2)}) async-start(), calls=%async_computation.2 | async-start | bytes 4456448 | tf_op jit(solution)/shard_map/reduce_scatter | solution.py:34
  49.2 2.0 copy-start
  57.3 164.1 %reduce-scatter.5.cloned.1.call-start = ((), (), s32[]{:S(2)}) async-start(), calls=%async_computation.3 | async-start | bytes 4456448 | tf_op jit(solution)/shard_map/reduce_scatter | solution.py:35
  57.3 92.2 %collective-permute-start = (bf16[1024,2048]{1,0:T(8,128)(2,1)}, bf16[1024,2048]{1,0:T(8,128)(2,1)S(1)}, u32[]{:S(2)}, u32[]{:S(2)}) collective-permute-start(bf16[1024,2048]{1,0:T(8,128)(2,1)} %copy-done), channel_id=1, source_target_pairs={{0,16},{16,32},{32,48},{48,64},{64,80},{80,96},{96,112},{112,128},... | collective-permute-start | bytes 12582920 | tf_op jit(solution)/shard_map/ppermute | solution.py:10
Sparse Core Ops, SparseCore 0:
  57.4 60.8 reduce-scatter.2
  158.0 63.3 reduce-scatter.4
where the time goes:
time: 230 us
  waiting for transfers between devices  151 us (66%)
  blocking collectives  28.8 us (13%)
  between operations  14.7 us (6%)
  other arithmetic  14.6 us (6%)
  matrix products  14.4 us (6%)
  local copies, waits for them, and re-layouts  3.2 us (1%)
  starting transfers between devices  3.19 us (1%)
    ppermute x1, waiting for transfers between devices, shifted(): lax.ppermute(value, axis, [(source, source + steps) for source in range(l...  89.1 us
    reduce_scatter x1, waiting for transfers between devices, on_device(): lax.psum_scatter(offdiag_part, 'pix', scatter_dimension=0, tiled=True)  61.8 us
    psum x1, blocking collectives, on_device(): frame_sums = lax.psum(jnp.sum(corrected, axis=1), 'pix')  28.8 us
    dot_general x2, matrix products, gram(): lax.dot_general(left, right, (((1,), (1,)), ((), ())), preferred_element_...  14.4 us
  transfers between devices with their start and end apart: 3, of which 2 were waited for; matrix products, arithmetic and copies ran while one was open for 4% of the time, Pallas kernels for 0%

commit v1 on v0

--- a/solution.py
+++ b/solution.py
@@ -2,6 +2,11 @@
 import jax.numpy as jnp
 from jax import lax
 from jax.sharding import PartitionSpec as P
+from jax.lax import all_gather
+
+
+def switch_values_by_axis(state):
+    return all_gather(state, "pix").sum(axis=0)
 
 
 def shifted(value, axis, steps):
@@ -24,7 +29,7 @@
     weights = flat_field * valid
     pixel_total = jnp.sum(owner_counts).astype(jnp.float32)
     corrected = photon_counts.astype(jnp.float32) * weights[None, :]
-    frame_sums = lax.psum(jnp.sum(corrected, axis=1), "pix")
+    frame_sums = switch_values_by_axis(jnp.sum(corrected, axis=1))
     frame_mean = frame_sums / pixel_total
     scaled = (corrected / frame_mean[:, None]).astype(jnp.bfloat16)
     earlier = shifted(scaled, "frames", 1)

time: 230 us -> 223 us (0.970)
  blocking collectives: 28.8 us -> 20.1 us
    psum x1 -> x0, blocking collectives: 28.8 us -> none  [on_device(): frame_sums = lax.psum(jnp.sum(corrected, axis=1), 'pix')]
    all_gather x0 -> x1, blocking collectives: none -> 20.1 us  [switch_values_by_axis(): return all_gather(state, 'pix').sum(axis=0)]
    ppermute x1, waiting for transfers between devices: 89.1 us -> 91.8 us  [shifted(): lax.ppermute(value, axis, [(source, source + steps) for source in range(l...]
  transfers between devices with their start and end apart: 3 -> 3, of which waited for: 2 -> 2; matrix products, arithmetic and copies ran while one was open for 4% -> 5% of each run, Pallas kernels for 0% -> 0%
where the time goes in v1:
time: 223 us; the launch traced here: 222 us
  waiting for transfers between devices  152 us (68%)
  blocking collectives  20.1 us (9%)
  between operations  14.7 us (7%)
  other arithmetic  14.6 us (7%)
  matrix products  14.4 us (6%)
  local copies, waits for them, and re-layouts  3.22 us (1%)
  starting transfers between devices  3.18 us (1%)
    ppermute x1, waiting for transfers between devices, shifted(): lax.ppermute(value, axis, [(source, source + steps) for source in range(l...  91.8 us
    reduce_scatter x1, waiting for transfers between devices, on_device(): lax.psum_scatter(offdiag_part, 'pix', scatter_dimension=0, tiled=True)  59.8 us
    all_gather x1, blocking collectives, switch_values_by_axis(): return all_gather(state, 'pix').sum(axis=0)  20.1 us
    dot_general x2, matrix products, gram(): lax.dot_general(left, right, (((1,), (1,)), ((), ())), preferred_element_...  14.4 us
  transfers between devices with their start and end apart: 3, of which 2 were waited for; matrix products, arithmetic and copies ran while one was open for 5% of the time, Pallas kernels for 0%

profile of v1, /device:TPU:4, one launch (start us, length us, event | category | flops | bytes accessed | tf_op | source)
XLA Modules:
  0.0 222.0 jit_solution(1555571836613258133)
XLA Ops:
  7.2 0.0 reduce-scatter.3.cloned.1.call-start
  7.2 1.3 reduce_sum.29
  8.5 1.2 dynamic_slice.3
  9.7 1.3 fusion.1
  11.1 4.3 %fusion = f32[1024]{0:T(1024)S(1)} fusion(s32[1024,2048]{1,0:T(8,128)} %param.3, f32[2048]{0:T(1024)S(1)} %fusion.1), kind=kLoop, calls=%fused_computation.2 | loop fusion | flops 6290432 | bytes 8400896 | tf_op jit(solution)/shard_map/reduce_sum | solution.py:32
  15.4 20.1 %all-gather = f32[16384]{0:T(1024)S(1)} all-gather(f32[1024]{0:T(1024)S(1)} %fusion), channel_id=2, replica_groups=mesh['frames'=16,'pix'=16] {'pix'}, dimensions={0}, use_global_device_ids=true | all-gather | bytes 69632 | tf_op jit(solution)/shard_map/all_gather | solution.py:9
  36.2 4.3 %divide_convert_fusion = bf16[1024,2048]{1,0:T(8,128)(2,1)S(1)} fusion(s32[1024,2048]{1,0:T(8,128)} %param.3, f32[1024]{0:T(1024)S(1)} %broadcast_divide_fusion.2, f32[2048]{0:T(1024)S(1)} %fusion.1), kind=kLoop, calls=%fused_computation | loop fusion | flops 8388608 | bytes 12595200 | tf_op jit(solution)/shard_map/convert_element_type | solution.py:34
  40.5 0.0 copy-start
  40.6 2.0 copy-done
  42.5 6.1 %fusion.2 = f32[1024,1024]{1,0:T(8,128)} fusion(bf16[1024,2048]{1,0:T(8,128)(2,1)S(1)} %divide_convert_fusion), kind=kOutput, calls=%fused_computation.8 | convolution fusion | flops 4294967296 | bytes 8388608 | tf_op jit(solution)/shard_map/dot_general | solution.py:19
  48.6 0.0 reduce-scatter.3.cloned.1.call-update
  48.6 0.0 reduce-scatter.5.cloned.1.call-start
  48.7 3.1 %collective-permute-start = (bf16[1024,2048]{1,0:T(8,128)(2,1)}, bf16[1024,2048]{1,0:T(8,128)(2,1)S(1)}, u32[]{:S(2)}, u32[]{:S(2)}) collective-permute-start(bf16[1024,2048]{1,0:T(8,128)(2,1)} %copy-done), channel_id=1, source_target_pairs={{0,16},{16,32},{32,48},{48,64},{64,80},{80,96},{96,112},{112,128},... | collective-permute-start | bytes 12582920 | tf_op jit(solution)/shard_map/ppermute | solution.py:15
  51.8 91.8 %collective-permute-done = bf16[1024,2048]{1,0:T(8,128)(2,1)S(1)} collective-permute-done((bf16[1024,2048]{1,0:T(8,128)(2,1)}, bf16[1024,2048]{1,0:T(8,128)(2,1)S(1)}, u32[]{:S(2)}, u32[]{:S(2)}) %collective-permute-start) | collective-permute-done | bytes 4194336 | tf_op jit(solution)/shard_map/ppermute | solution.py:15
  143.6 8.4 %fusion.3 = f32[1024,1024]{1,0:T(8,128)} fusion(bf16[1024,2048]{1,0:T(8,128)(2,1)} %copy-done, bf16[1024,2048]{1,0:T(8,128)(2,1)S(1)} %collective-permute-done), kind=kOutput, calls=%fused_computation.9 | convolution fusion | flops 4294967296 | bytes 12582912 | tf_op jit(solution)/shard_map/dot_general | solution.py:19
  152.0 0.0 reduce-scatter.5.cloned.1.call-update
  152.0 0.0 reduce-scatter.3.cloned.1.call-done
  152.0 1.7 broadcast_divide_fusion.1
  153.7 59.8 %reduce-scatter.5.cloned.1.call-done = f32[64,1024]{1,0:T(8,128)} async-done(((f32[1024,1024]{1,0:T(8,128)}), f32[64,1024]{1,0:T(8,128)}) %reduce-scatter.5.cloned.1.call-update) | async-done | bytes 262160 | tf_op jit(solution)/shard_map/reduce_scatter | solution.py:40
  213.5 1.7 broadcast_divide_fusion
  (3 shorter events, 0.0 us)
Async XLA Ops:
  7.2 144.9 %reduce-scatter.3.cloned.1.call-start = ((), (), s32[]{:S(2)}) async-start(), calls=%async_computation.2 | async-start | bytes 4456448 | tf_op jit(solution)/shard_map/reduce_scatter | solution.py:39
  40.5 2.0 copy-start
  48.6 164.8 %reduce-scatter.5.cloned.1.call-start = ((), (), s32[]{:S(2)}) async-start(), calls=%async_computation.3 | async-start | bytes 4456448 | tf_op jit(solution)/shard_map/reduce_scatter | solution.py:40
  48.7 94.9 %collective-permute-start = (bf16[1024,2048]{1,0:T(8,128)(2,1)}, bf16[1024,2048]{1,0:T(8,128)(2,1)S(1)}, u32[]{:S(2)}, u32[]{:S(2)}) collective-permute-start(bf16[1024,2048]{1,0:T(8,128)(2,1)} %copy-done), channel_id=1, source_target_pairs={{0,16},{16,32},{32,48},{48,64},{64,80},{80,96},{96,112},{112,128},... | collective-permute-start | bytes 12582920 | tf_op jit(solution)/shard_map/ppermute | solution.py:15
Sparse Core Ops, SparseCore 0:
  48.8 61.3 reduce-scatter.2
  152.1 61.3 reduce-scatter.4
